TPU v7x, 32 devices: a whole 2x2x4 slice. The times are simulated.
32 devices in a mesh: expert: 8 (over z, y), replica: 4 (over x, core).
Axes of the slice: x: 2, y: 2, z: 4, core: 2. Of those that a mesh axis runs over, the one named last changes fastest.
Arguments:
- tokens: bfloat16 [4096, 2048], P(('expert', 'replica')), may hold values from -6 to 6
- expert_ids: int32 [4096, 8], P(('expert', 'replica')), may hold values from 0 to 31, as said below
- gates: float32 [4096, 8], P(('expert', 'replica')), may hold values from 0.02 to 0.25
- cotangent: bfloat16 [4096, 2048], P(('expert', 'replica')), may hold values from -6 to 6
- expert_weights: bfloat16 [32, 2048, 1152], P(('expert', 'replica')), may hold values from -0.125 to 0.125
- moment_first: bfloat16 [32, 2048, 1152], P(('expert', 'replica')), may hold values from -0.00021362305 to 0.00021362305
- moment_second: bfloat16 [32, 2048, 1152], P(('expert', 'replica')), may hold values from 1.3242243e-09 to 1.3213139e-08
- hot_slot: int32 [8], P('expert'), may hold values from 0 to 3
Outputs:
- mixed: bfloat16 [4096, 2048], P(('expert', 'replica'))
- input_grad: bfloat16 [4096, 2048], P(('expert', 'replica'))
- gate_grad: float32 [4096, 8], P(('expert', 'replica'))
- new_weights: bfloat16 [32, 2048, 1152], P(('expert', 'replica'))
- hot_copy: bfloat16 [32, 2048, 1152], P(('expert', 'replica'))
Inputs may be any that keep to these rules, and one draw needn't show every extreme that they name: `expert_ids`: each token names 8 different experts. Experts form 8 groups of 4 consecutive numbers. Of the choices of the 128 tokens of one device (aligned blocks of rows), exactly 128 name experts of each group; in group a the expert a * 4 + hot_slot[a] is named exactly 64 times, every other expert at most 32 times, and one of them exactly 32 times.
All inputs are finite; a program needn't handle non-finite values.
Results may differ from a plain program's by a relative error of at most 0.011.
Values may be sent and summed in bfloat16 or wider, within the bound.
No kernel may reach another device: no remote copies, remote signals or barrier semaphores. Data moves between devices by JAX's collectives and lax.ppermute only.
A program may use at most 256 MiB of HBM per device.

v0:
```python
import jax
import jax.numpy as jnp
from jax import lax
from jax.sharding import PartitionSpec as P

beta_first = 0.9
beta_second = 0.95
adam_eps = 1e-08
rate = 0.05
clip_norm = 1.0
bias_first = 1.0 - 0.9**10
bias_second = 1.0 - 0.95**10


def broadcast(value, axis, source):
    kept = jnp.where(lax.axis_index(axis) == source, value, 0).astype(value.dtype)
    return lax.psum(kept, axis)


def expert_forward(row_block, weights, hidden_width):
    gate_up = jnp.dot(row_block, weights[:, : 2 * hidden_width], preferred_element_type=jnp.float32)
    gate_in = gate_up[:, :hidden_width]
    up_part = gate_up[:, hidden_width:]
    hidden = (gate_in * jax.nn.sigmoid(gate_in) * up_part).astype(jnp.bfloat16)
    outputs = lax.dot_general(
        hidden,
        weights[:, 2 * hidden_width :],
        (((1,), (1,)), ((), ())),
        preferred_element_type=jnp.float32,
    ).astype(jnp.bfloat16)
    return (outputs, gate_up, hidden)


def expert_backward(cot_block, gate_up, weights, hidden_width):
    gate_in = gate_up[:, :hidden_width]
    up_part = gate_up[:, hidden_width:]
    sigmoid_gate = jax.nn.sigmoid(gate_in)
    hidden_grad = jnp.dot(
        cot_block, weights[:, 2 * hidden_width :], preferred_element_type=jnp.float32
    )
    grad_gate = hidden_grad * up_part * sigmoid_gate * (1.0 + gate_in * (1.0 - sigmoid_gate))
    grad_up = hidden_grad * gate_in * sigmoid_gate
    input_both = jnp.concatenate([grad_gate, grad_up], axis=1).astype(jnp.bfloat16)
    slot_grads = lax.dot_general(
        input_both,
        weights[:, : 2 * hidden_width],
        (((1,), (1,)), ((), ())),
        preferred_element_type=jnp.float32,
    ).astype(jnp.bfloat16)
    return (slot_grads, input_both)


def partial_sums(row_block, cot_block, input_both, hidden, leading):
    in_part = jnp.einsum(
        "arcd,arcg->rdg",
        row_block.reshape(leading + (-1,)),
        input_both.reshape(leading + (-1,)),
        preferred_element_type=jnp.float32,
    )
    down_part = jnp.einsum(
        "arcd,arcf->rdf",
        cot_block.reshape(leading + (-1,)),
        hidden.reshape(leading + (-1,)),
        preferred_element_type=jnp.float32,
    )
    partial_value = lax.optimization_barrier(
        jnp.concatenate([in_part, down_part], axis=2).astype(jnp.bfloat16)
    )
    return jnp.sum(partial_value.astype(jnp.float32), axis=0)


def place_slots(target, bins, room, allowed):
    one_hot = (target[:, None] == jnp.arange(bins, dtype=jnp.int32)[None, :]).astype(
        jnp.int32
    ) * allowed[:, None].astype(jnp.int32)
    ahead = jnp.cumsum(one_hot, axis=0) - one_hot
    return target * room + jnp.sum(ahead * one_hot, axis=1)


def to_experts(row_block):
    return lax.all_to_all(row_block, ("expert", "replica"), split_axis=0, concat_axis=0, tiled=True)


def from_experts(row_block):
    return lax.all_to_all(row_block, ("expert", "replica"), split_axis=0, concat_axis=0, tiled=True)


def shards(
    tokens, expert_ids, gates, cotangent, expert_weights, moment_first, moment_second, hot_slot
):
    groups = lax.axis_size("expert")
    owners = lax.axis_size("replica")
    experts = groups * owners
    token_count, chosen = expert_ids.shape
    slot_total = token_count * chosen
    hidden_width = expert_weights.shape[2] // 3
    capacity = 2 * slot_total // experts
    weights = expert_weights[0]
    routed = expert_ids.reshape(-1)
    slot_numbers = jnp.arange(slot_total, dtype=jnp.int32)
    zero_half = jnp.zeros((), jnp.bfloat16)
    all_true = jnp.ones((slot_total,), jnp.bool_)
    hot_member = hot_slot[0]
    slot_place = place_slots(routed, experts, capacity, all_true)
    slot_source = jnp.zeros((experts * capacity,), jnp.int32).at[slot_place].set(slot_numbers)
    slot_filled = jnp.zeros((experts * capacity,), jnp.bool_).at[slot_place].set(True)
    arrived = to_experts(jnp.where(slot_filled[:, None], tokens[slot_source // chosen], zero_half))
    outputs, gate_up, hidden = expert_forward(arrived, weights, hidden_width)
    slot_out = from_experts(outputs)[slot_place]
    slot_wide = slot_out.astype(jnp.float32).reshape(token_count, chosen, -1)
    mixed = jnp.einsum("tk,tkd->td", gates, slot_wide).astype(jnp.bfloat16)
    gate_grad = jnp.einsum("td,tkd->tk", cotangent.astype(jnp.float32), slot_wide)
    slot_cot = (
        (gates[:, :, None] * cotangent[:, None, :].astype(jnp.float32))
        .astype(jnp.bfloat16)
        .reshape(slot_total, -1)
    )
    cot_arrived = to_experts(jnp.where(slot_filled[:, None], slot_cot[slot_source], zero_half))
    slot_grads, input_both = expert_backward(cot_arrived, gate_up, weights, hidden_width)
    gradient = partial_sums(arrived, cot_arrived, input_both, hidden, (groups, owners, capacity))
    slot_dx = from_experts(slot_grads)[slot_place]
    input_grad = jnp.sum(
        slot_dx.astype(jnp.float32).reshape(token_count, chosen, -1), axis=1
    ).astype(jnp.bfloat16)
    clip_bound = clip_norm * experts ** (-0.5)
    scale = jnp.minimum(1.0, clip_bound / (jnp.sqrt(jnp.sum(gradient * gradient)) + 1e-06))
    scaled = scale * gradient
    first = beta_first * moment_first[0].astype(jnp.float32) + (1.0 - beta_first) * scaled
    second = (
        beta_second * moment_second[0].astype(jnp.float32) + (1.0 - beta_second) * scaled * scaled
    )
    update = first / bias_first / (jnp.sqrt(second / bias_second) + adam_eps)
    new_weights = (weights.astype(jnp.float32) - rate * update).astype(jnp.bfloat16)
    hot_copy = broadcast(new_weights, "replica", hot_member)
    return (mixed, input_grad, gate_grad, new_weights[None], hot_copy[None])


def solution(mesh):
    return jax.shard_map(
        shards,
        mesh=mesh,
        in_specs=(
            P(("expert", "replica"), None),
            P(("expert", "replica"), None),
            P(("expert", "replica"), None),
            P(("expert", "replica"), None),
            P(("expert", "replica"), None, None),
            P(("expert", "replica"), None, None),
            P(("expert", "replica"), None, None),
            P("expert"),
        ),
        out_specs=(
            P(("expert", "replica"), None),
            P(("expert", "replica"), None),
            P(("expert", "replica"), None),
            P(("expert", "replica"), None, None),
            P(("expert", "replica"), None, None),
        ),
        check_vma=False,
    )
```

profile of v0, /device:TPU:0, one launch (start us, length us, event | category | flops | bytes accessed | tf_op | source)
XLA Modules:
  0.0 949.9 jit_solution(18028048421142596829)
XLA Ops:
  8.9 9.0 reduce-window.6
  31.9 19.1 %gather_fusion.2 = bf16[2048,2048]{1,0:T(8,128)(2,1)} fusion(bf16[1024,2048]{1,0:T(8,128)(2,1)} %fusion.19, s32[2048]{0:T(1024)S(1)} %get-tuple-element.13), kind=kCustom, calls=%fused_computation.2 | custom fusion | bytes 16785408 | tf_op jit(solution)/shard_map/gather | solution.py:118
  51.0 11.0 %gather_fusion = bf16[2048,2048]{1,0:T(8,128)(2,1)} fusion(bf16[128,2048]{1,0:T(8,128)(2,1)S(1)} %copy-done, s32[2048]{0:T(1024)S(1)} %get-tuple-element.14), kind=kCustom, calls=%fused_computation | custom fusion | bytes 16785408 | tf_op jit(solution)/shard_map/gather | solution.py:107
  62.0 9.2 broadcast_select_fusion
  71.2 190.7 %all_to_all.42 = bf16[32,64,2048]{2,1,0:T(8,128)(2,1)} all-to-all(bf16[32,64,2048]{2,1,0:T(8,128)(2,1)S(1)} %get-tuple-element.16), channel_id=1, replica_groups=mesh['expert'=8,'replica'=4] {'expert','replica'}, dimensions={0} | all-to-all | bytes 16777216 | tf_op jit(solution)/shard_map/all_to_all | solution.py:81
  272.8 11.8 %fusion.31 = f32[2048,768]{1,0:T(8,128)} fusion(bf16[2048,2048]{1,0:T(8,128)(2,1)} %bitcast.101, bf16[2048,1152]{0,1:T(8,128)(2,1)} %bitcast.94), kind=kOutput, calls=%fused_computation.59 | convolution fusion | flops 6442450944 | bytes 17825792 | tf_op jit(solution)/shard_map/dot_general | solution.py:21
  284.6 167.6 %all-to-all-done.2 = bf16[32,64,2048]{2,1,0:T(8,128)(2,1)} async-done(((bf16[32,64,2048]{2,1,0:T(8,128)(2,1)}), bf16[32,64,2048]{2,1,0:T(8,128)(2,1)}, u32[]{:S(2)}, u32[]{:S(2)}) %all-to-all-start.2) | async-done | bytes 8388640 | tf_op jit(solution)/shard_map/all_to_all | solution.py:81
  452.2 12.8 %multiply_convert_fusion.1 = (bf16[2048,384]{1,0:T(8,128)(2,1)S(1)}, bf16[2048,384]{1,0:T(8,128)(2,1)S(1)}, bf16[2048,384]{1,0:T(8,128)(2,1)}) fusion(f32[2048,768]{1,0:T(8,128)} %fusion.31, bf16[2048,2048]{1,0:T(8,128)(2,1)} %bitcast.14, bf16[2048,1152]{0,1:T(8,128)(2,1)} %bitcast.95), kind=kOutput, calls=%fused_computation.55 | convolution fusion | flops 3233808384 | bytes 20971520 | tf_op jit(solution)/shard_map/dot_general | solution.py:38
  465.0 9.0 convolution_convert_fusion
  474.0 14.4 %all-to-all-start.3 = ((bf16[32,64,2048]{2,1,0:T(8,128)(2,1)}), bf16[32,64,2048]{2,1,0:T(8,128)(2,1)}, u32[]{:S(2)}, u32[]{:S(2)}) async-start(bf16[32,64,2048]{2,1,0:T(8,128)(2,1)} %bitcast.103), calls=%async_computation.3 | async-start | bytes 16777216 | tf_op jit(solution)/shard_map/all_to_all | solution.py:85
  488.4 9.8 %convolution_convert_fusion.1 = bf16[2048,2048]{1,0:T(8,128)(2,1)} fusion(bf16[2048,384]{1,0:T(8,128)(2,1)} %get-tuple-element.12, bf16[2048,1152]{0,1:T(8,128)(2,1)} %bitcast.96), kind=kOutput, calls=%fused_computation.41 | convolution fusion | flops 3225419776 | bytes 11534336 | tf_op jit(solution)/shard_map/dot_general | solution.py:25
  498.1 176.3 %all-to-all-done.3 = bf16[32,64,2048]{2,1,0:T(8,128)(2,1)} async-done(((bf16[32,64,2048]{2,1,0:T(8,128)(2,1)}), bf16[32,64,2048]{2,1,0:T(8,128)(2,1)}, u32[]{:S(2)}, u32[]{:S(2)}) %all-to-all-start.3) | async-done | bytes 8388640 | tf_op jit(solution)/shard_map/all_to_all | solution.py:85
  678.2 6.7 copy.35
  692.4 9.9 %bitcast_convert_fusion.1 = bf16[4,2048,384]{1,2,0:T(8,128)(2,1)} fusion(bf16[8,4,64,2048]{3,2,1,0:T(8,128)(2,1)} %bitcast.24, bf16[8,4,64,384]{3,2,1,0:T(8,128)(2,1)} %bitcast.116), kind=kOutput, calls=%fused_computation.11 | convolution fusion | flops 3224371200 | bytes 16252928 | tf_op jit(solution)/shard_map/arcd,arcf->rdf/dot_general | solution.py:60
  702.3 12.4 %bitcast_convert_fusion = bf16[4,2048,768]{1,2,0:T(8,128)(2,1)} fusion(bf16[8,4,64,2048]{3,2,1,0:T(8,128)(2,1)} %bitcast.102, bf16[8,4,64,384]{3,2,1,0:T(8,128)(2,1)} %bitcast.115, bf16[8,4,64,384]{3,2,1,0:T(8,128)(2,1)S(1)} %bitcast.114), kind=kOutput, calls=%fused_computation.7 | convolution fusion | flops 6455033856 | bytes 24117248 | tf_op jit(solution)/shard_map/arcd,arcg->rdg/dot_general | solution.py:54
  714.7 20.3 %pad_maximum_fusion = bf16[4,2048,1152]{1,2,0:T(8,128)(2,1)} fusion(bf16[4,2048,384]{1,2,0:T(8,128)(2,1)} %bitcast_convert_fusion.1, bf16[4,2048,768]{1,2,0:T(8,128)(2,1)} %bitcast_convert_fusion), kind=kLoop, calls=%fused_computation.8 | loop fusion | flops 37748736 | bytes 37748736 | tf_op jit(solution)/shard_map/concatenate | solution.py:67
  735.0 14.7 %convert_reduce_fusion = f32[2048,1152]{0,1:T(8,128)} fusion(bf16[4,2048,1152]{1,2,0:T(8,128)(2,1)} %pad_maximum_fusion), kind=kLoop, calls=%fused_computation.6 | loop fusion | flops 16515072 | bytes 28311552 | tf_op jit(solution)/shard_map/reduce_sum | solution.py:69
  749.7 6.8 multiply_reduce_fusion
  757.2 14.3 %select_bitcast_fusion = bf16[1,2048,1152]{1,2,0:T(8,128)(2,1)} fusion(pred[]{:T(512)S(6)} %eq.36, bf16[1,2048,1152]{1,2,0:T(8,128)(2,1)} %copy.36, f32[2048,1152]{0,1:T(8,128)} %convert_reduce_fusion, f32[]{:T(128)S(6)} %min.3, bf16[1,2048,1152]{1,2,0:T(8,128)(2,1)} %copy.35, bf16[1,2048,1152]{1,2,0:T(8,128)(2,1)} %copy.32), kind=kLoop, calls=%fused_computation.42 | loop fusion | flops 44826624 | bytes 28311556 | tf_op jit(solution)/shard_map/broadcast_in_dim | solution.py:135
  771.5 14.5 %fusion.18 = bf16[1,2048,1152]{1,2,0:T(8,128)(2,1)} fusion(bf16[1,2048,1152]{1,2,0:T(8,128)(2,1)} %copy.36, bf16[1,2048,1152]{1,2,0:T(8,128)(2,1)} %copy.35, bf16[1,2048,1152]{1,2,0:T(8,128)(2,1)} %copy.32, f32[2048,1152]{0,1:T(8,128)} %convert_reduce_fusion, f32[]{:T(128)S(6)} %min.3), kind=kLoop, calls=%fused_computation.35 | loop fusion | flops 42467328 | bytes 28311556 | tf_op jit(solution)/shard_map/convert_element_type | solution.py:133
  786.1 6.6 copy.37
  792.7 102.5 %all-reduce.2.cloned.1.call-done = bf16[1,2048,1152]{1,2,0:T(8,128)(2,1)} async-done(((bf16[1,2048,1152]{1,2,0:T(8,128)(2,1)}), bf16[1,2048,1152]{1,2,0:T(8,128)(2,1)}) %all-reduce.2.cloned.1.call-update) | async-done | bytes 4718608 | tf_op jit(solution)/shard_map/psum | solution.py:17
  901.9 13.5 %gather_fusion.3 = bf16[1024,2048]{1,0:T(8,128)(2,1)} fusion(bf16[2048,2048]{1,0:T(8,128)(2,1)} %bitcast.16, s32[1024]{0:T(1024)S(1)} %broadcast_clamp_fusion), kind=kCustom, calls=%fused_computation.3 | custom fusion | bytes 8392704 | tf_op jit(solution)/shard_map/gather | solution.py:121
  921.3 13.3 %gather_fusion.1 = bf16[1024,2048]{1,0:T(8,128)(2,1)} fusion(bf16[2048,2048]{1,0:T(8,128)(2,1)} %bitcast.8, s32[1024]{0:T(1024)S(1)} %broadcast_clamp_fusion), kind=kCustom, calls=%fused_computation.1 | custom fusion | bytes 8392704 | tf_op jit(solution)/shard_map/gather | solution.py:109
  (54 shorter events, 57.6 us)
Async XLA Ops:
  7.2 43.8 %copy-start = (bf16[128,2048]{1,0:T(8,128)(2,1)S(1)}, bf16[128,2048]{1,0:T(8,128)(2,1)}, u32[]{:S(2)}) copy-start(bf16[128,2048]{1,0:T(8,128)(2,1)} %param.8) | copy-start | bytes 1572868
  261.9 190.3 %all-to-all-start.2 = ((bf16[32,64,2048]{2,1,0:T(8,128)(2,1)}), bf16[32,64,2048]{2,1,0:T(8,128)(2,1)}, u32[]{:S(2)}, u32[]{:S(2)}) async-start(bf16[32,64,2048]{2,1,0:T(8,128)(2,1)} %get-tuple-element.15), calls=%async_computation.2 | async-start | bytes 16777216 | tf_op jit(solution)/shard_map/all_to_all | solution.py:81
  452.2 12.8 %copy-start.2 = (bf16[1,2048,1152]{1,2,0:T(8,128)(2,1)S(1)}, bf16[1,2048,1152]{1,2,0:T(8,128)(2,1)}, u32[]{:S(2)}) copy-start(bf16[1,2048,1152]{1,2,0:T(8,128)(2,1)} %copy.32) | copy-start | bytes 14155780
  465.0 9.0 copy-start.6
  474.0 200.5 %all-to-all-start.3 = ((bf16[32,64,2048]{2,1,0:T(8,128)(2,1)}), bf16[32,64,2048]{2,1,0:T(8,128)(2,1)}, u32[]{:S(2)}, u32[]{:S(2)}) async-start(bf16[32,64,2048]{2,1,0:T(8,128)(2,1)} %bitcast.103), calls=%async_computation.3 | async-start | bytes 16777216 | tf_op jit(solution)/shard_map/all_to_all | solution.py:85
  674.5 246.8 %all-to-all-start.1 = ((bf16[32,64,2048]{2,1,0:T(8,128)(2,1)}), bf16[32,64,2048]{2,1,0:T(8,128)(2,1)}, u32[]{:S(2)}, u32[]{:S(2)}) async-start(bf16[32,64,2048]{2,1,0:T(8,128)(2,1)} %bitcast.100), calls=%async_computation.1 | async-start | bytes 16777216 | tf_op jit(solution)/shard_map/all_to_all | solution.py:85
  678.2 217.1 %all-reduce.2.cloned.1.call-start = ((), (), s32[]{:S(2)}) async-start(), calls=%async_computation.4 | async-start | bytes 9437184 | tf_op jit(solution)/shard_map/psum | solution.py:17
  685.0 7.3 copy-start.5
  934.6 4.7 copy-start.3
  934.6 4.7 copy-start.4
  934.6 8.0 copy-start.1
Sparse Core Ops, SparseCore 0:
  771.7 123.5 all-reduce.1
where the time goes:
time: 958 us; the launch traced here: 950 us
  waiting for transfers between devices  446 us (47%)
  blocking collectives  191 us (20%)
  local copies, waits for them, and re-layouts  103 us (11%)
  other arithmetic  99.2 us (10%)
  matrix products  71.9 us (8%)
  starting transfers between devices  22.4 us (2%)
  between operations  16 us (2%)
    all_to_all x1, blocking collectives, to_experts(): lax.all_to_all(row_block, ('expert', 'replica'), split_axis=0, concat_axi...  191 us
    all_to_all x2, waiting for transfers between devices, from_experts(): lax.all_to_all(row_block, ('expert', 'replica'), split_axis=0, concat_axi...  176 us
    all_to_all x1, waiting for transfers between devices, to_experts(): lax.all_to_all(row_block, ('expert', 'replica'), split_axis=0, concat_axi...  168 us
    psum x1, waiting for transfers between devices, broadcast(): return lax.psum(kept, axis)  103 us
    unnamed x22, local copies, waits for them, and re-layouts  35 us
    concatenate x1, other arithmetic, partial_sums(): jnp.concatenate([in_part, down_part], axis=2).astype(jnp.bfloat16)  20.3 us
  transfers between devices with their start and end apart: 4, of which 3 were waited for; matrix products, arithmetic and copies ran while one was open for 18% of the time, Pallas kernels for 0%

commit v1 on v0

--- a/solution.py
+++ b/solution.py
@@ -14,7 +14,7 @@
 
 def broadcast(value, axis, source):
     kept = jnp.where(lax.axis_index(axis) == source, value, 0).astype(value.dtype)
-    return lax.psum(kept, axis)
+    return jnp.sum(lax.all_gather(kept, axis), axis=0)
 
 
 def expert_forward(row_block, weights, hidden_width):

time: 958 us -> 910 us (0.950)
  waiting for transfers between devices: 446 us -> 410 us
  starting transfers between devices: 22.4 us -> 11.9 us
    psum x1 -> x0, waiting for transfers between devices: 103 us -> none  [broadcast(): return lax.psum(kept, axis)]
    all_to_all x2, waiting for transfers between devices: 176 us -> 257 us  [from_experts(): lax.all_to_all(row_block, ('expert', 'replica'), split_axis=0, concat_axi...]
    select_n x0 -> x1, other arithmetic: none -> 16.3 us  [broadcast(): jnp.where(lax.axis_index(axis) == source, value, 0).astype(value.dtype)]
    convert_element_type x1 -> x0, other arithmetic: 14.5 us -> none  [shards(): (weights.astype(jnp.float32) - rate * update).astype(jnp.bfloat16)]
    broadcast_in_dim x1 -> x0, other arithmetic: 14.3 us -> none  [shards(): return (mixed, input_grad, gate_grad, new_weights[None], hot_copy[None])]
    all_to_all x1, waiting for transfers between devices: 168 us -> 154 us  [to_experts(): lax.all_to_all(row_block, ('expert', 'replica'), split_axis=0, concat_axi...]
    reduce_sum x0 -> x1, other arithmetic: none -> 13.3 us  [broadcast(): return jnp.sum(lax.all_gather(kept, axis), axis=0)]
    all_to_all x2, starting transfers between devices: 18.1 us -> 7.69 us  [from_experts(): lax.all_to_all(row_block, ('expert', 'replica'), split_axis=0, concat_axi...]
  transfers between devices with their start and end apart: 4 -> 4, of which waited for: 3 -> 3; matrix products, arithmetic and copies ran while one was open for 18% -> 19% of each run, Pallas kernels for 0% -> 0%
where the time goes in v1:
time: 910 us; the launch traced here: 901 us
  waiting for transfers between devices  410 us (45%)
  blocking collectives  191 us (21%)
  local copies, waits for them, and re-layouts  103 us (11%)
  other arithmetic  99.8 us (11%)
  matrix products  69.7 us (8%)
  between operations  15.9 us (2%)
  starting transfers between devices  11.9 us (1%)
    all_to_all x2, waiting for transfers between devices, from_experts(): lax.all_to_all(row_block, ('expert', 'replica'), split_axis=0, concat_axi...  257 us
    all_to_all x1, blocking collectives, to_experts(): lax.all_to_all(row_block, ('expert', 'replica'), split_axis=0, concat_axi...  191 us
    all_to_all x1, waiting for transfers between devices, to_experts(): lax.all_to_all(row_block, ('expert', 'replica'), split_axis=0, concat_axi...  154 us
    unnamed x29, local copies, waits for them, and re-layouts  28.5 us
    concatenate x1, other arithmetic, partial_sums(): jnp.concatenate([in_part, down_part], axis=2).astype(jnp.bfloat16)  20.3 us
    gather x1, local copies, waits for them, and re-layouts, shards(): slot_cot[slot_source]  19 us
  transfers between devices with their start and end apart: 4, of which 3 were waited for; matrix products, arithmetic and copies ran while one was open for 19% of the time, Pallas kernels for 0%

profile of v1, /device:TPU:0, one launch (start us, length us, event | category | flops | bytes accessed | tf_op | source)
XLA Modules:
  0.0 901.3 jit_solution(9103542177026335327)
XLA Ops:
  8.9 9.0 %reduce-window.6 = s32[32,8,128]{2,1,0:T(8,128)S(1)} reduce-window(s32[32,8,128]{2,1,0:T(8,128)S(1)} %fusion.31, s32[]{:T(128)} %constant.17.clone.1), window={size=1x1x128 pad=0_0x0_0x127_0}, to_apply=%region_0.0 | reduce-window | flops 4161536 | bytes 262148 | tf_op jit(solution)/shard_map/reduce-window
  31.9 19.0 %gather_fusion.2 = bf16[2048,2048]{1,0:T(8,128)(2,1)} fusion(bf16[1024,2048]{1,0:T(8,128)(2,1)} %fusion.10, s32[2048]{0:T(1024)S(1)} %get-tuple-element.15), kind=kCustom, calls=%fused_computation.2 | custom fusion | bytes 16785408 | tf_op jit(solution)/shard_map/gather | solution.py:118
  51.0 11.0 %gather_fusion = bf16[2048,2048]{1,0:T(8,128)(2,1)} fusion(bf16[128,2048]{1,0:T(8,128)(2,1)S(1)} %copy-done, s32[2048]{0:T(1024)S(1)} %get-tuple-element.16), kind=kCustom, calls=%fused_computation | custom fusion | bytes 16785408 | tf_op jit(solution)/shard_map/gather | solution.py:107
  62.0 9.2 %broadcast_select_fusion = (bf16[32,64,2048]{2,1,0:T(8,128)(2,1)}, bf16[32,64,2048]{2,1,0:T(8,128)(2,1)S(1)}) fusion(bf16[32,64,2048]{2,1,0:T(8,128)(2,1)} %bitcast.77, pred[32,64]{1,0:T(8,128)(4,1)S(1)} %broadcast_in_dim.49, bf16[32,64,2048]{2,1,0:T(8,128)(2,1)} %bitcast.78), kind=kLoop, calls=%fused_computation.25 | loop fusion | flops 8388608 | bytes 33556480 | tf_op jit(solution)/shard_map/jit(_where)/select_n | solution.py:118
  71.2 190.7 %all_to_all.42 = bf16[32,64,2048]{2,1,0:T(8,128)(2,1)} all-to-all(bf16[32,64,2048]{2,1,0:T(8,128)(2,1)S(1)} %get-tuple-element.18), channel_id=1, replica_groups=mesh['expert'=8,'replica'=4] {'expert','replica'}, dimensions={0} | all-to-all | bytes 16777216 | tf_op jit(solution)/shard_map/all_to_all | solution.py:81
  266.1 6.7 copy.33
  286.7 11.7 %fusion.22 = f32[2048,768]{1,0:T(8,128)} fusion(bf16[2048,2048]{1,0:T(8,128)(2,1)} %bitcast.80, bf16[2048,1152]{1,0:T(8,128)(2,1)} %bitcast.84), kind=kOutput, calls=%fused_computation.46 | convolution fusion | flops 6442450944 | bytes 17825792 | tf_op jit(solution)/shard_map/dot_general | solution.py:21
  298.5 153.7 %all-to-all-done.2 = bf16[32,64,2048]{2,1,0:T(8,128)(2,1)} async-done(((bf16[32,64,2048]{2,1,0:T(8,128)(2,1)}), bf16[32,64,2048]{2,1,0:T(8,128)(2,1)}, u32[]{:S(2)}, u32[]{:S(2)}) %all-to-all-start.2) | async-done | bytes 8388640 | tf_op jit(solution)/shard_map/all_to_all | solution.py:81
  452.2 11.6 %multiply_convert_fusion.1 = (bf16[2048,384]{1,0:T(8,128)(2,1)S(1)}, bf16[2048,384]{1,0:T(8,128)(2,1)S(1)}, bf16[2048,384]{1,0:T(8,128)(2,1)S(1)}) fusion(f32[2048,768]{1,0:T(8,128)} %fusion.22, bf16[2048,2048]{1,0:T(8,128)(2,1)} %bitcast.14, bf16[2048,1152]{1,0:T(8,128)(2,1)} %bitcast.85), kind=kOutput, calls=%fused_computation.42 | convolution fusion | flops 3233808384 | bytes 20971520 | tf_op jit(solution)/shard_map/dot_general | solution.py:38
  463.9 9.0 convolution_convert_fusion
  476.6 9.6 %bitcast_convert_fusion.1 = bf16[4,2048,384]{1,2,0:T(8,128)(2,1)} fusion(bf16[8,4,64,2048]{3,2,1,0:T(8,128)(2,1)} %bitcast.24, bf16[8,4,64,384]{3,2,1,0:T(8,128)(2,1)S(1)} %bitcast.100), kind=kOutput, calls=%fused_computation.10 | convolution fusion | flops 3224371200 | bytes 16252928 | tf_op jit(solution)/shard_map/arcd,arcf->rdf/dot_general | solution.py:60
  486.2 13.2 %bitcast_convert_fusion = bf16[4,2048,768]{1,2,0:T(8,128)(2,1)} fusion(bf16[8,4,64,2048]{3,2,1,0:T(8,128)(2,1)} %bitcast.81, bf16[8,4,64,384]{3,2,1,0:T(8,128)(2,1)} %bitcast.102, bf16[8,4,64,384]{3,2,1,0:T(8,128)(2,1)} %bitcast.101), kind=kOutput, calls=%fused_computation.7 | convolution fusion | flops 6455033856 | bytes 24117248 | tf_op jit(solution)/shard_map/arcd,arcg->rdg/dot_general | solution.py:54
  499.3 20.3 %pad_maximum_fusion = bf16[4,2048,1152]{1,2,0:T(8,128)(2,1)} fusion(bf16[4,2048,384]{1,2,0:T(8,128)(2,1)} %bitcast_convert_fusion.1, bf16[4,2048,768]{1,2,0:T(8,128)(2,1)} %bitcast_convert_fusion), kind=kLoop, calls=%fused_computation.8 | loop fusion | flops 37748736 | bytes 37748736 | tf_op jit(solution)/shard_map/concatenate | solution.py:67
  519.6 14.6 %convert_reduce_fusion = f32[2048,1152]{0,1:T(8,128)} fusion(bf16[4,2048,1152]{1,2,0:T(8,128)(2,1)} %pad_maximum_fusion), kind=kLoop, calls=%fused_computation.6 | loop fusion | flops 16515072 | bytes 28311552 | tf_op jit(solution)/shard_map/reduce_sum | solution.py:69
  534.2 6.7 multiply_reduce_fusion
  541.6 16.3 %broadcast_select_fusion.2 = (bf16[1,2048,1152]{1,2,0:T(8,128)(2,1)}, bf16[1,2048,1152]{1,2,0:T(8,128)(2,1)}) fusion(pred[]{:T(512)S(6)} %eq.36, bf16[1,2048,1152]{1,2,0:T(8,128)(2,1)} %copy.35, f32[2048,1152]{0,1:T(8,128)} %convert_reduce_fusion, f32[]{:T(128)S(6)} %min.3, bf16[1,2048,1152]{1,2,0:T(8,128)(2,1)} %copy.34, bf16[1,2048,1152]{1,2,0:T(8,128)(2,1)} %copy.33), kind=kLoop, calls=%fused_computation.29 | loop fusion | flops 44826624 | bytes 33030148 | tf_op jit(solution)/shard_map/jit(_where)/select_n | solution.py:16
  557.9 6.7 copy.36
  564.6 8.4 convolution_convert_fusion.1
  573.0 89.9 %all-to-all-done.3 = bf16[32,64,2048]{2,1,0:T(8,128)(2,1)} async-done(((bf16[32,64,2048]{2,1,0:T(8,128)(2,1)}), bf16[32,64,2048]{2,1,0:T(8,128)(2,1)}, u32[]{:S(2)}, u32[]{:S(2)}) %all-to-all-start.3) | async-done | bytes 8388640 | tf_op jit(solution)/shard_map/all_to_all | solution.py:85
  667.0 6.7 copy.37
  673.7 13.3 %gather_fusion.3 = bf16[1024,2048]{1,0:T(8,128)(2,1)} fusion(bf16[2048,2048]{1,0:T(8,128)(2,1)} %bitcast.16, s32[1024]{0:T(1024)S(1)} %broadcast_clamp_fusion), kind=kCustom, calls=%fused_computation.3 | custom fusion | bytes 8392704 | tf_op jit(solution)/shard_map/gather | solution.py:121
  687.0 166.7 %all-to-all-done.1 = bf16[32,64,2048]{2,1,0:T(8,128)(2,1)} async-done(((bf16[32,64,2048]{2,1,0:T(8,128)(2,1)}), bf16[32,64,2048]{2,1,0:T(8,128)(2,1)}, u32[]{:S(2)}, u32[]{:S(2)}) %all-to-all-start.1) | async-done | bytes 8388640 | tf_op jit(solution)/shard_map/all_to_all | solution.py:85
  853.7 13.3 %gather_fusion.1 = bf16[1024,2048]{1,0:T(8,128)(2,1)} fusion(bf16[2048,2048]{1,0:T(8,128)(2,1)} %bitcast.8, s32[1024]{0:T(1024)S(1)} %broadcast_clamp_fusion), kind=kCustom, calls=%fused_computation.1 | custom fusion | bytes 8392704 | tf_op jit(solution)/shard_map/gather | solution.py:109
  880.9 13.3 %reduce_sum.58 = bf16[2048,1152]{1,0:T(8,128)(2,1)} reduce(bf16[4,2048,1152]{2,1,0:T(8,128)(2,1)} %all-gather.2.cloned.1.call-done, bf16[]{:T(256)} %constant.23.clone.1), dimensions={0}, to_apply=%region_8.9 | reduce | flops 7077888 | bytes 23592962 | tf_op jit(solution)/shard_map/reduce_sum | solution.py:17
  (63 shorter events, 54.9 us)
Async XLA Ops:
  7.2 43.8 %copy-start = (bf16[128,2048]{1,0:T(8,128)(2,1)S(1)}, bf16[128,2048]{1,0:T(8,128)(2,1)}, u32[]{:S(2)}) copy-start(bf16[128,2048]{1,0:T(8,128)(2,1)} %param.8) | copy-start | bytes 1572868
  18.7 32.3 %copy-start.5 = (s32[1024,1]{0,1:T(1,128)}, s32[1024,1]{0,1:T(1,128)S(1)}, u32[]{:S(2)}) copy-start(s32[1024,1]{0,1:T(1,128)S(1)} %compare_select_fusion) | copy-start | bytes 12292
  262.0 190.2 %all-to-all-start.2 = ((bf16[32,64,2048]{2,1,0:T(8,128)(2,1)}), bf16[32,64,2048]{2,1,0:T(8,128)(2,1)}, u32[]{:S(2)}, u32[]{:S(2)}) async-start(bf16[32,64,2048]{2,1,0:T(8,128)(2,1)} %get-tuple-element.17), calls=%async_computation.2 | async-start | bytes 16777216 | tf_op jit(solution)/shard_map/all_to_all | solution.py:81
  286.7 177.1 %slice-start = ((s8[4718592]{0:T(1024)(128)(4,1)}), s8[524288]{0:T(1024)(128)(4,1)S(1)}, s32[]{:S(2)}) async-start(s8[4718592]{0:T(1024)(128)(4,1)} %bitcast.87), calls=%async_computation.5 | async-start | bytes 1048576
  452.2 11.7 %slice-start.1 = ((s8[4718592]{0:T(1024)(128)(4,1)}), s8[4194304]{0:T(1024)(128)(4,1)S(1)}, s32[]{:S(2)}) async-start(s8[4718592]{0:T(1024)(128)(4,1)} %bitcast.87), calls=%async_computation.6 | async-start | bytes 8388608
  463.8 9.0 %copy-start.7 = (bf16[2048,384]{1,0:T(8,128)(2,1)}, bf16[2048,384]{1,0:T(8,128)(2,1)S(1)}, u32[]{:S(2)}) copy-start(bf16[2048,384]{1,0:T(8,128)(2,1)S(1)} %get-tuple-element.12) | copy-start | bytes 4718596
  463.8 9.0 %copy-start.8 = (bf16[2048,384]{1,0:T(8,128)(2,1)}, bf16[2048,384]{1,0:T(8,128)(2,1)S(1)}, u32[]{:S(2)}) copy-start(bf16[2048,384]{1,0:T(8,128)(2,1)S(1)} %get-tuple-element.13) | copy-start | bytes 4718596
  472.9 190.0 %all-to-all-start.3 = ((bf16[32,64,2048]{2,1,0:T(8,128)(2,1)}), bf16[32,64,2048]{2,1,0:T(8,128)(2,1)}, u32[]{:S(2)}, u32[]{:S(2)}) async-start(bf16[32,64,2048]{2,1,0:T(8,128)(2,1)} %bitcast.79), calls=%async_computation.3 | async-start | bytes 16777216 | tf_op jit(solution)/shard_map/all_to_all | solution.py:85
  476.6 404.3 %all-gather.2.cloned.1.call-start = ((), (), s32[]{:S(2)}) async-start(), calls=%async_computation.4 | async-start | bytes 23592960 | tf_op jit(solution)/shard_map/all_gather | solution.py:17
  662.8 4.0 copy-start.4
  662.8 4.2 copy-start.6
  662.8 190.8 %all-to-all-start.1 = ((bf16[32,64,2048]{2,1,0:T(8,128)(2,1)}), bf16[32,64,2048]{2,1,0:T(8,128)(2,1)}, u32[]{:S(2)}, u32[]{:S(2)}) async-start(bf16[32,64,2048]{2,1,0:T(8,128)(2,1)} %bitcast.82), calls=%async_computation.1 | async-start | bytes 16777216 | tf_op jit(solution)/shard_map/all_to_all | solution.py:85
  866.9 4.7 copy-start.2
  866.9 4.7 copy-start.3
  875.0 19.3 %copy-start.1 = (bf16[128,2048]{1,0:T(8,128)(2,1)S(1)}, bf16[128,2048]{1,0:T(8,128)(2,1)}, u32[]{:S(2)}) copy-start(bf16[128,2048]{1,0:T(8,128)(2,1)} %param.8) | copy-start | bytes 1572868
Sparse Core Ops, SparseCore 0:
  564.7 211.6 all-gather.1
